TPU v7x, 32 devices: a whole 2x2x4 slice. The times are simulated.
32 devices in a mesh: dp: 2 (over x), mp: 16 (over z, y, core).
Axes of the slice: x: 2, y: 2, z: 4, core: 2. Of those that a mesh axis runs over, the one named last changes fastest.
Arguments:
- tokens: bfloat16 [32, 512, 768], P(('dp', 'mp')), may hold values from -6 to 6
- segment_ids: int32 [32, 512], P(('dp', 'mp')), may hold values from 0 to 3, never falling along the last dimension, each value on 1 to 256 neighbouring positions
- swap_step: int32 [1], replicated, may hold values from 0 to 1023
- feature_bank: bfloat16 [8, 12, 64, 64], replicated, may hold values from -5 to 5
- query_weight: bfloat16 [768, 768], replicated, may hold values from -0.21875 to 0.21875
- query_bias: bfloat16 [768], replicated, may hold values from -1.5 to 1.5
- key_weight: bfloat16 [768, 768], replicated, may hold values from -0.21875 to 0.21875
- value_weight: bfloat16 [768, 768], replicated, may hold values from -0.21875 to 0.21875
- value_bias: bfloat16 [768], replicated, may hold values from -1.5 to 1.5
- out_weight: bfloat16 [768, 768], replicated, may hold values from -0.875 to 0.875
- out_bias: bfloat16 [768], replicated, may hold values from -1.5 to 1.5
- position_logits: bfloat16 [12, 1023], replicated, may hold values from -3 to 3
- first_gain: bfloat16 [768], replicated, may hold values from 0.5 to 1.5
- first_shift: bfloat16 [768], replicated, may hold values from -1.5 to 1.5
- up_weight: bfloat16 [768, 3072], P(None, 'mp'), may hold values from -0.21875 to 0.21875
- up_bias: bfloat16 [3072], P('mp'), may hold values from -1.5 to 1.5
- down_weight: bfloat16 [3072, 768], P('mp'), may hold values from -0.109375 to 0.109375
- down_bias: bfloat16 [768], replicated, may hold values from -1.5 to 1.5
- second_gain: bfloat16 [768], replicated, may hold values from 0.5 to 1.5
- second_shift: bfloat16 [768], replicated, may hold values from -1.5 to 1.5
- out_cotangent: bfloat16 [32, 512, 768], P(('dp', 'mp')), may hold values from -6 to 6
Outputs:
- layer_out: bfloat16 [32, 512, 768], P(('dp', 'mp'))
- grad_tokens: float32 [32, 512, 768], P(('dp', 'mp'))
- grad_query_weight: float32 [768, 768], replicated
- grad_query_bias: float32 [768], replicated
- grad_key_weight: float32 [768, 768], replicated
- grad_value_weight: float32 [768, 768], replicated
- grad_value_bias: float32 [768], replicated
- grad_out_weight: float32 [768, 768], replicated
- grad_out_bias: float32 [768], replicated
- grad_position_logits: float32 [12, 1023], replicated
- grad_first_gain: float32 [768], replicated
- grad_first_shift: float32 [768], replicated
- grad_up_weight: float32 [768, 3072], P(None, 'mp')
- grad_up_bias: float32 [3072], P('mp')
- grad_down_weight: float32 [3072, 768], P('mp')
- grad_down_bias: float32 [768], replicated
- grad_second_gain: float32 [768], replicated
- grad_second_shift: float32 [768], replicated
Inputs may be any that keep to these rules, and one draw needn't show every extreme that they name: `segment_ids`: within each row the ids never fall; a document holds at most 256 tokens.
All inputs are finite; a program needn't handle non-finite values.
Results may differ from a plain program's by a relative error of at most 0.02.
Values may be sent and summed in bfloat16 or wider, within the bound.
No kernel may reach another device: no remote copies, remote signals or barrier semaphores. Data moves between devices by JAX's collectives and lax.ppermute only.
A program may use at most 320 MiB of HBM per device.

v0:
```python
import jax
import jax.numpy as jnp
from jax import lax
from jax.sharding import PartitionSpec as P

EPSILON = 1e-05


def dot_first(left_side, right_side):
    return lax.dot_general(
        left_side, right_side, (((0,), (0,)), ((), ())), preferred_element_type=jnp.float32
    )


def dot_last(left_side, right_side):
    return lax.dot_general(
        left_side, right_side, (((1,), (1,)), ((), ())), preferred_element_type=jnp.float32
    )


def toeplitz(entries):
    head_count, span = entries.shape
    length = (span + 1) // 2
    rolled = jnp.roll(entries[:, ::-1], length, axis=1)
    tiled = jnp.tile(rolled, (1, length))[:, : length * (span - 1)]
    return tiled.reshape(head_count, length, span - 1)[:, :, :length]


def normalize(inputs, factor, offset):
    centre = inputs - jnp.mean(inputs, axis=-1, keepdims=True)
    spread = jnp.mean(centre * centre, axis=-1, keepdims=True)
    inverse = lax.rsqrt(spread + EPSILON)
    normed = centre * inverse
    return (normed * factor + offset, normed, inverse)


def norm_back(upstream, normed, inverse, factor):
    scaled = upstream * factor
    inner = (
        scaled
        - jnp.mean(scaled, axis=-1, keepdims=True)
        - normed * jnp.mean(scaled * normed, axis=-1, keepdims=True)
    )
    return (inverse * inner, jnp.sum(upstream * normed, axis=0), jnp.sum(upstream, axis=0))


def lift(row_block, projection):
    lifted = jnp.einsum("lhd,hdm->hlm", row_block, projection, preferred_element_type=jnp.float32)
    widened = row_block.astype(jnp.float32)
    squares = jnp.einsum("lhd,lhd->hl", widened, widened)
    return jnp.exp(lifted - 0.5 * squares[:, :, None]) * projection.shape[-1] ** (-0.5)


def lift_back(row_block, projection, feature, grad_feature):
    product = grad_feature.astype(jnp.float32) * feature
    rounded = product.astype(jnp.bfloat16)
    through = jnp.einsum("hlm,hdm->lhd", rounded, projection, preferred_element_type=jnp.float32)
    return through - row_block.astype(jnp.float32) * jnp.sum(product, axis=-1).T[:, :, None]


def row_scores(row_queries, row_keys, row_values, row_segments, projection, position_table):
    query_feat = lift(row_queries, projection)
    key_feat = lift(row_keys, projection)
    query_low = query_feat.astype(jnp.bfloat16)
    key_low = key_feat.astype(jnp.bfloat16)
    same_doc = (row_segments[:, None] == row_segments[None, :]).astype(jnp.float32)
    kernel = jnp.einsum("hlm,hkm->hlk", query_low, key_low, preferred_element_type=jnp.float32)
    weights = kernel * position_table * same_doc[None]
    denominator = jnp.sum(weights, axis=-1)
    weights_low = weights.astype(jnp.bfloat16)
    numerator = jnp.einsum(
        "hlk,khd->lhd", weights_low, row_values, preferred_element_type=jnp.float32
    )
    return (
        query_feat,
        key_feat,
        query_low,
        key_low,
        same_doc,
        kernel,
        weights_low,
        denominator,
        numerator,
    )


def local(
    tokens,
    segment_ids,
    swap_step,
    feature_bank,
    query_weight,
    query_bias,
    key_weight,
    value_weight,
    value_bias,
    out_weight,
    out_bias,
    position_logits,
    first_gain,
    first_shift,
    up_weight,
    up_bias,
    down_weight,
    down_bias,
    second_gain,
    second_shift,
    out_cotangent,
):
    rows_here, length, model_width = tokens.shape
    head_count = position_logits.shape[0]
    head_size = model_width // head_count
    query_scale = head_size ** (-0.25)
    token_rows = tokens.reshape(-1, model_width)
    projection = lax.dynamic_index_in_dim(
        feature_bank, swap_step[0] % feature_bank.shape[0], 0, keepdims=False
    )
    entries = jnp.exp(position_logits.astype(jnp.float32))
    position_table = toeplitz(entries)

    def by_heads(array):
        return array.reshape(rows_here, length, head_count, head_size)

    queries = (
        (
            jnp.dot(token_rows, query_weight, preferred_element_type=jnp.float32)
            + query_bias.astype(jnp.float32)
        )
        * query_scale
    ).astype(jnp.bfloat16)
    keys_all = (
        jnp.dot(token_rows, key_weight, preferred_element_type=jnp.float32) * query_scale
    ).astype(jnp.bfloat16)
    values = (
        jnp.dot(token_rows, value_weight, preferred_element_type=jnp.float32)
        + value_bias.astype(jnp.float32)
    ).astype(jnp.bfloat16)

    def forward_row(pieces):
        row_queries, row_keys, row_values, row_segments = pieces
        scores = row_scores(
            row_queries, row_keys, row_values, row_segments, projection, position_table
        )
        return (scores[8] / scores[7].T[:, :, None]).astype(jnp.bfloat16)

    mixed_out = lax.map(
        forward_row, (by_heads(queries), by_heads(keys_all), by_heads(values), segment_ids)
    ).reshape(-1, model_width)
    branch = jnp.dot(mixed_out, out_weight, preferred_element_type=jnp.float32) + out_bias.astype(
        jnp.float32
    )
    first_factor = first_gain.astype(jnp.float32)
    hidden, first_normed, first_inverse = normalize(
        token_rows.astype(jnp.float32) + branch, first_factor, first_shift.astype(jnp.float32)
    )
    hidden_low = hidden.astype(jnp.bfloat16)
    gathered = lax.all_gather(hidden_low, "mp", axis=0, tiled=True)
    upward = jnp.dot(gathered, up_weight, preferred_element_type=jnp.float32) + up_bias.astype(
        jnp.float32
    )
    activated = jax.nn.gelu(upward, approximate=False).astype(jnp.bfloat16)
    feed_out = lax.psum_scatter(
        jnp.dot(activated, down_weight, preferred_element_type=jnp.float32),
        "mp",
        scatter_dimension=0,
        tiled=True,
    )
    second_factor = second_gain.astype(jnp.float32)
    summed = hidden + feed_out + down_bias.astype(jnp.float32)
    layer_out, second_normed, second_inverse = normalize(
        summed, second_factor, second_shift.astype(jnp.float32)
    )
    upstream = out_cotangent.reshape(-1, model_width).astype(jnp.float32)
    grad_summed, grad_second_gain, grad_second_shift = norm_back(
        upstream, second_normed, second_inverse, second_factor
    )
    grad_down_bias = jnp.sum(grad_summed, axis=0)
    grad_feed = grad_summed.astype(jnp.bfloat16)

    def gelu_exact(inputs):
        return jax.nn.gelu(inputs, approximate=False)

    grad_gathered = lax.all_gather(grad_feed, "mp", axis=0, tiled=True)
    grad_act = dot_last(grad_gathered, down_weight)
    grad_upward = jax.vjp(gelu_exact, upward)[1](grad_act)[0].astype(jnp.bfloat16)
    part_up_weight = dot_first(gathered, grad_upward)
    part_down_weight = dot_first(activated, grad_gathered)
    part_up_bias = jnp.sum(grad_upward.astype(jnp.float32), axis=0)
    grad_hidden_ffn = lax.psum_scatter(
        dot_last(grad_upward, up_weight), "mp", scatter_dimension=0, tiled=True
    )
    grad_up_weight, grad_up_bias, grad_down_weight = lax.psum(
        (part_up_weight, part_up_bias, part_down_weight), "dp"
    )
    grad_hidden = grad_summed + grad_hidden_ffn
    grad_residual, grad_first_gain, grad_first_shift = norm_back(
        grad_hidden, first_normed, first_inverse, first_factor
    )
    grad_branch = grad_residual.astype(jnp.bfloat16)
    grad_out_bias = jnp.sum(grad_branch.astype(jnp.float32), axis=0)
    grad_out_weight = dot_first(mixed_out, grad_branch)
    grad_mixed = dot_last(grad_branch, out_weight).astype(jnp.bfloat16)

    def backward_row(running, pieces):
        row_queries, row_keys, row_values, row_segments, row_grad = pieces
        (
            query_feat,
            key_feat,
            query_low,
            key_low,
            same_doc,
            kernel,
            weights_low,
            denominator,
            numerator,
        ) = row_scores(row_queries, row_keys, row_values, row_segments, projection, position_table)
        spread_denom = denominator.T[:, :, None]
        grad_wide = row_grad.astype(jnp.float32)
        grad_numer = (grad_wide / spread_denom).astype(jnp.bfloat16)
        grad_denom = -jnp.einsum("lhd,lhd->hl", grad_wide, numerator / spread_denom) / denominator
        grad_weights = (
            jnp.einsum("lhd,khd->hlk", grad_numer, row_values, preferred_element_type=jnp.float32)
            + grad_denom[:, :, None]
        )
        grad_values = jnp.einsum(
            "hlk,lhd->khd", weights_low, grad_numer, preferred_element_type=jnp.float32
        ).astype(jnp.bfloat16)
        masked = grad_weights * same_doc[None]
        grad_kernel = (masked * position_table).astype(jnp.bfloat16)
        running = running + masked * kernel
        grad_qfeat = jnp.einsum(
            "hlk,hkm->hlm", grad_kernel, key_low, preferred_element_type=jnp.float32
        ).astype(jnp.bfloat16)
        grad_kfeat = jnp.einsum(
            "hlk,hlm->hkm", grad_kernel, query_low, preferred_element_type=jnp.float32
        ).astype(jnp.bfloat16)
        grad_queries = lift_back(row_queries, projection, query_feat, grad_qfeat).astype(
            jnp.bfloat16
        )
        grad_keys = lift_back(row_keys, projection, key_feat, grad_kfeat).astype(jnp.bfloat16)
        return (running, (grad_queries, grad_keys, grad_values))

    start_table = jnp.zeros((head_count, length, length), jnp.float32)
    table_grad, row_grads = lax.scan(
        backward_row,
        start_table,
        (
            by_heads(queries),
            by_heads(keys_all),
            by_heads(values),
            segment_ids,
            by_heads(grad_mixed),
        ),
    )
    grad_queries = row_grads[0].reshape(-1, model_width)
    grad_keys = row_grads[1].reshape(-1, model_width)
    grad_values = row_grads[2].reshape(-1, model_width)
    grad_query_weight = dot_first(token_rows, grad_queries) * query_scale
    grad_query_bias = jnp.sum(grad_queries.astype(jnp.float32), axis=0) * query_scale
    grad_key_weight = dot_first(token_rows, grad_keys) * query_scale
    grad_value_weight = dot_first(token_rows, grad_values)
    grad_value_bias = jnp.sum(grad_values.astype(jnp.float32), axis=0)
    grad_tokens = (
        grad_residual
        + query_scale * (dot_last(grad_queries, query_weight) + dot_last(grad_keys, key_weight))
        + dot_last(grad_values, value_weight)
    )
    toeplitz_back = jax.vjp(toeplitz, entries)[1]
    grad_logits = toeplitz_back(table_grad)[0] * entries
    shared = lax.psum(
        (
            grad_query_weight,
            grad_query_bias,
            grad_key_weight,
            grad_value_weight,
            grad_value_bias,
            grad_out_weight,
            grad_out_bias,
            grad_logits,
            grad_first_gain,
            grad_first_shift,
            grad_down_bias,
            grad_second_gain,
            grad_second_shift,
        ),
        ("dp", "mp"),
    )
    return (
        layer_out.astype(jnp.bfloat16).reshape(rows_here, length, model_width),
        grad_tokens.reshape(rows_here, length, model_width),
        shared[0],
        shared[1],
        shared[2],
        shared[3],
        shared[4],
        shared[5],
        shared[6],
        shared[7],
        shared[8],
        shared[9],
        grad_up_weight,
        grad_up_bias,
        grad_down_weight,
        shared[10],
        shared[11],
        shared[12],
    )


def solution(mesh):
    in_specs = (
        P(("dp", "mp"), None, None),
        P(("dp", "mp"), None),
        P(),
        P(),
        P(),
        P(),
        P(),
        P(),
        P(),
        P(),
        P(),
        P(),
        P(),
        P(),
        P(None, "mp"),
        P("mp"),
        P("mp", None),
        P(),
        P(),
        P(),
        P(("dp", "mp"), None, None),
    )
    out_specs = (
        P(("dp", "mp"), None, None),
        P(("dp", "mp"), None, None),
        P(),
        P(),
        P(),
        P(),
        P(),
        P(),
        P(),
        P(),
        P(),
        P(),
        P(None, "mp"),
        P("mp"),
        P("mp", None),
        P(),
        P(),
        P(),
    )
    return jax.shard_map(local, mesh=mesh, in_specs=in_specs, out_specs=out_specs, check_vma=False)
```

profile of v0, /device:TPU:8, one launch (start us, length us, event | category | flops | bytes accessed | tf_op | source)
XLA Modules:
  0.0 1372.5 jit_solution(12590324390042866375)
XLA Ops:
  20.0 11.5 tile.4
  31.5 38.0 %tile.10 = f32[12,523776]{1,0:T(8,128)} reshape(f32[12,512,1023]{2,1,0:T(8,128)} %tile.4) | data formatting | bytes 50282496 | tf_op jit(solution)/shard_map/tile | solution.py:25
  69.5 22.6 %slice.28 = f32[12,523264]{1,0:T(8,128)} slice(f32[12,523776]{1,0:T(8,128)} %tile.10), slice={[0:12], [0:523264]} | slice | bytes 50233344 | tf_op jit(solution)/shard_map/slice | solution.py:25
  92.1 42.2 %reshape.182 = f32[12,512,1022]{2,1,0:T(8,128)} reshape(f32[12,523264]{1,0:T(8,128)} %slice.28) | data formatting | bytes 50233344 | tf_op jit(solution)/shard_map/reshape | solution.py:26
  134.3 10.7 slice.29
  145.0 12.6 copy.112
  166.5 9.4 fusion.7
  182.2 100.6 %all-gather.3.cloned.1.call-done = bf16[8192,768]{1,0:T(8,128)(2,1)} async-done(((bf16[512,768]{1,0:T(8,128)(2,1)}), bf16[8192,768]{1,0:T(8,128)(2,1)}) %all-gather.3.cloned.1.call-update) | async-done | bytes 12582928 | tf_op jit(solution)/shard_map/all_gather | solution.py:157
  282.8 20.5 %multiply_convert_fusion.1 = (bf16[8192,192]{0,1:T(8,128)(2,1)S(1)}, f32[8192,192]{0,1:T(8,128)}, f32[8192,192]{0,1:T(8,128)}) fusion(f32[192]{0:T(256)S(1)} %convert_element_type.196, bf16[8192,768]{1,0:T(8,128)(2,1)} %all-gather.3.cloned.1.call-done, bf16[768,192]{0,1:T(8,128)(2,1)} %param.35), kind=kOutput, calls=%fused_computation.9 | convolution fusion | flops 2519728128 | bytes 28607232 | tf_op jit(solution)/shard_map/dot_general | solution.py:158
  305.1 10.1 fusion.63
  315.9 240.6 %reduce-scatter.3.cloned.1.call-done = f32[512,768]{1,0:T(8,128)} async-done(((f32[8192,768]{1,0:T(8,128)}), f32[512,768]{1,0:T(8,128)}) %reduce-scatter.3.cloned.1.call-update) | async-done | bytes 1572880 | tf_op jit(solution)/shard_map/reduce_scatter | solution.py:162
  565.2 100.3 %all-gather.5.cloned.1.call-done = bf16[8192,768]{1,0:T(8,128)(2,1)} async-done(((bf16[512,768]{1,0:T(8,128)(2,1)}), bf16[8192,768]{1,0:T(8,128)(2,1)}) %all-gather.5.cloned.1.call-update) | async-done | bytes 12582928 | tf_op jit(solution)/shard_map/all_gather | solution.py:183
  665.5 10.9 convert_reduce_fusion
  678.1 10.1 fusion.64
  688.7 240.8 %reduce-scatter.5.cloned.1.call-done = f32[512,768]{1,0:T(8,128)} async-done(((f32[8192,768]{1,0:T(8,128)}), f32[512,768]{1,0:T(8,128)}) %reduce-scatter.5.cloned.1.call-update) | async-done | bytes 1572880 | tf_op jit(solution)/shard_map/reduce_scatter | solution.py:189
  940.1 5.7 convert_reduce_fusion.3
  945.8 18.3 %fusion = (f32[12,512,512]{1,2,0:T(8,128)}, bf16[12,512,512]{1,2,0:T(8,128)(2,1)}) fusion(f32[12,512,512]{1,2,0:T(8,128)} %get-tuple-element.152, f32[12,512]{1,0:T(8,128)S(1)} %negate_divide_fusion, f32[512,512]{0,1:T(8,128)} %compare_convert_fusion, f32[12,512,512]{1,2,0:T(8,128)} %copy.112, bf16[512,12,64]{0,2,1:T(8,128)(2,1)} %bitcast.162, ...), kind=kOutput, calls=%fused_computation.3 | convolution fusion | flops 419561472 | bytes 46710784 | tf_op jit(solution)/shard_map/while/body/eval_jaxpr/lhd,khd->hlk/dot_general | solution.py:222
  964.1 4.1 fusion.61
  980.9 5.6 psum.123
  986.5 9.4 fusion.67
  995.9 8.2 fusion.68
  1004.2 12.8 copy.113
  1017.0 14.6 %pad.14.clone = f32[12,512,1022]{2,1,0:T(8,128)} pad(f32[12,512,512]{2,1,0:T(8,128)} %copy.113, f32[]{:T(128)} %constant.51.clone.1), padding=0_0x0_0x0_510 | pad | bytes 37699588 | tf_op jit(solution)/shard_map/transpose(jvp())/pad | solution.py:26
  1031.6 47.0 %reshape.189 = f32[12,523264]{1,0:T(8,128)} reshape(f32[12,512,1022]{2,1,0:T(8,128)} %pad.14.clone) | data formatting | bytes 50233344 | tf_op jit(solution)/shard_map/transpose(jvp())/reshape | solution.py:26
  1078.6 22.9 %pad.15 = f32[12,523776]{1,0:T(8,128)} pad(f32[12,523264]{1,0:T(8,128)} %reshape.189, f32[]{:T(128)} %constant.51.clone.1), padding=0_0x0_512 | pad | bytes 50257924 | tf_op jit(solution)/shard_map/transpose(jvp())/pad | solution.py:25
  1101.5 43.8 %reshape.190 = f32[12,512,1023]{2,1,0:T(8,128)} reshape(f32[12,523776]{1,0:T(8,128)} %pad.15) | data formatting | bytes 50282496 | tf_op jit(solution)/shard_map/transpose(jvp())/reshape | solution.py:25
  1145.4 9.2 reduce_sum.214
  1157.3 3.4 fusion.66
  1162.7 4.5 add_bitcast_fusion
  1167.3 3.8 all-reduce.13.cloned.1.call-done
  1180.2 36.7 %all-reduce.15.cloned.1.call-done = (f32[768,192]{0,1:T(8,128)}, f32[192,768]{1,0:T(8,128)}) async-done(((f32[768,192]{0,1:T(8,128)}, f32[192,768]{1,0:T(8,128)}), (f32[768,192]{0,1:T(8,128)}, f32[192,768]{1,0:T(8,128)})) %all-reduce.15.cloned.1.call-update) | async-done | bytes 1179664 | tf_op jit(solution)/shard_map/psum | solution.py:192
  1216.9 136.8 %all-reduce.11.cloned.1.call-done = (f32[768]{0:T(1024)}, f32[768]{0:T(1024)}, f32[768]{0:T(1024)}, f32[12,1023]{1,0:T(8,128)}, f32[768]{0:T(1024)}, /*index=5*/...) async-done(((f32[768]{0:T(1024)}, f32[768]{0:T(1024)}, f32[768]{0:T(1024)}, f32[12,1023]{1,0:T(8,128)}, f32[768]{0:T(1024)}, /*index=5*/f32[768]{0:T(1024)}, ...) | async-done | bytes 73696 | tf_op jit(solution)/shard_map/psum | solution.py:270
  (209 shorter events, 89.0 us)
Async XLA Ops:
  7.2 157.0 %copy-start = (bf16[8,12,64,64]{3,2,1,0:T(8,128)(2,1)S(1)}, bf16[8,12,64,64]{3,2,1,0:T(8,128)(2,1)}, u32[]{:S(2)}) copy-start(bf16[8,12,64,64]{3,2,1,0:T(8,128)(2,1)} %param.24) | copy-start | bytes 2359300
  7.2 275.6 %all-gather.3.cloned.1.call-start = ((), (), s32[]{:S(2)}) async-start(), calls=%async_computation.2 | async-start | bytes 13369344 | tf_op jit(solution)/shard_map/all_gather | solution.py:157
  8.8 3.9 copy-start.34
  14.2 150.0 %copy-start.9 = (bf16[512,768]{0,1:T(8,128)(2,1)}, bf16[512,768]{0,1:T(8,128)(2,1)S(1)}, u32[]{:S(2)}) copy-start(bf16[512,768]{0,1:T(8,128)(2,1)S(1)} %copy.58) | copy-start | bytes 2359300
  18.8 145.9 %copy-start.11 = (bf16[512,768]{0,1:T(8,128)(2,1)}, bf16[512,768]{0,1:T(8,128)(2,1)S(1)}, u32[]{:S(2)}) copy-start(bf16[512,768]{0,1:T(8,128)(2,1)S(1)} %copy.60) | copy-start | bytes 2359300
  145.0 12.6 copy-start.37
  145.0 13.7 copy-start.44
  164.7 11.2 copy-start.2
  166.5 9.4 copy-start.4
  166.5 9.4 copy-start.26
  182.1 374.4 %reduce-scatter.3.cloned.1.call-start = ((), (), s32[]{:S(2)}) async-start(), calls=%async_computation.3 | async-start | bytes 26738688 | tf_op jit(solution)/shard_map/reduce_scatter | solution.py:162
  182.1 123.0 %copy-start.32 = (bf16[192,768]{1,0:T(8,128)(2,1)S(1)}, bf16[192,768]{1,0:T(8,128)(2,1)}, u32[]{:S(2)}) copy-start(bf16[192,768]{1,0:T(8,128)(2,1)} %param.37) | copy-start | bytes 884740
  315.2 350.3 %all-gather.5.cloned.1.call-start = ((), (), s32[]{:S(2)}) async-start(), calls=%async_computation.4 | async-start | bytes 13369344 | tf_op jit(solution)/shard_map/all_gather | solution.py:183
  565.2 364.3 %reduce-scatter.5.cloned.1.call-start = ((), (), s32[]{:S(2)}) async-start(), calls=%async_computation.5 | async-start | bytes 26738688 | tf_op jit(solution)/shard_map/reduce_scatter | solution.py:189
  665.5 12.5 copy-start.33
  688.2 482.9 %all-reduce.13.cloned.1.call-start = ((), (), s32[]{:S(2)}) async-start(), calls=%async_computation.7 | async-start | bytes 18874368 | tf_op jit(solution)/shard_map/psum | solution.py:270
  938.1 7.7 copy-start.16
  945.8 18.3 %copy-start.3 = (f32[12,512,64]{1,2,0:T(8,128)S(1)}, f32[12,512,64]{1,2,0:T(8,128)}, u32[]{:S(2)}) copy-start(f32[12,512,64]{1,2,0:T(8,128)} %copy-done.2) | copy-start | bytes 4718596
  945.8 18.3 %copy-start.5 = (f32[12,512,64]{1,2,0:T(8,128)S(1)}, f32[12,512,64]{1,2,0:T(8,128)}, u32[]{:S(2)}) copy-start(f32[12,512,64]{1,2,0:T(8,128)} %copy-done.4) | copy-start | bytes 4718596
  964.1 4.6 copy-start.1
  979.1 237.9 %all-reduce.15.cloned.1.call-start = ((), (), s32[]{:S(2)}) async-start(), calls=%async_computation.8 | async-start | bytes 2359296 | tf_op jit(solution)/shard_map/psum | solution.py:192
  986.5 9.4 copy-start.23
  1004.1 349.6 %all-reduce.11.cloned.1.call-start = ((), (), s32[]{:S(2)}) async-start(), calls=%async_computation.6 | async-start | bytes 196608 | tf_op jit(solution)/shard_map/psum | solution.py:270
  1145.4 11.2 copy-start.35
  1157.3 3.4 copy-start.53
  1356.3 3.9 copy-start.36
  1356.3 4.6 copy-start.42
  1356.3 5.2 copy-start.41
  1356.3 5.7 copy-start.31
  1359.6 4.1 copy-start.40
  1359.6 4.7 copy-start.39
  1359.6 5.3 copy-start.38
  (32 other events, 57.4 us)
Sparse Core Ops, SparseCore 0:
  182.2 100.5 all-gather.2
  315.3 241.1 reduce-scatter.2
  565.3 100.1 all-gather.4
  688.3 241.0 reduce-scatter.4
  979.2 191.8 all-reduce.12
  1173.9 42.9 all-reduce.14
  1225.0 128.6 all-reduce.10
where the time goes:
time: 1380 us; the launch traced here: 1370 us
  waiting for transfers between devices  860 us (62%)
  local copies, waits for them, and re-layouts  320 us (23%)
  matrix products  142 us (10%)
  other arithmetic  28.3 us (2%)
  between operations  15.7 us (1%)
    reduce_scatter x1, waiting for transfers between devices, local(): lax.psum_scatter(dot_last(grad_upward, up_weight), 'mp', scatter_dimensio...  241 us
    reduce_scatter x1, waiting for transfers between devices, local(): lax.psum_scatter(jnp.dot(activated, down_weight, preferred_element_type=j...  241 us
    psum x2, waiting for transfers between devices, local(): lax.psum((grad_query_weight, grad_query_bias, grad_key_weight, grad_value...  141 us
    all_gather x1, waiting for transfers between devices, local(): gathered = lax.all_gather(hidden_low, 'mp', axis=0, tiled=True)  101 us
    all_gather x1, waiting for transfers between devices, local(): grad_gathered = lax.all_gather(grad_feed, 'mp', axis=0, tiled=True)  100 us
    reshape x2, local copies, waits for them, and re-layouts, toeplitz(): return tiled.reshape(head_count, length, span - 1)[:, :, :length]  89.2 us
    unnamed x130, local copies, waits for them, and re-layouts  59.4 us
    another operation x2, local copies, waits for them, and re-layouts, toeplitz(): tiled = jnp.tile(rolled, (1, length))[:, :length * (span - 1)]  49.6 us
  transfers between devices with their start and end apart: 7, of which 7 were waited for; matrix products, arithmetic and copies ran while one was open for 14% of the time, Pallas kernels for 0%

commit v1 on v0

v1 whole, which is shorter than its diff:
```python
import functools
import jax
import jax.numpy as jnp
from jax import lax
from jax.experimental import pallas as pl
from jax.experimental.pallas import tpu as pltpu
from jax.sharding import PartitionSpec as P

LANES = 128
LOW = jnp.bfloat16


def dot_last(left_side, right_side):
    return lax.dot_general(
        left_side, right_side, (((1,), (1,)), ((), ())), preferred_element_type=jnp.float32
    )


def dot_first(left_side, right_side):
    return lax.dot_general(
        left_side, right_side, (((0,), (0,)), ((), ())), preferred_element_type=jnp.float32
    )


def split_low(wide):
    high = wide.astype(LOW)
    return high, (wide - high.astype(jnp.float32)).astype(LOW)


def key_span(block, blocks, reach):
    first = max(0, block - reach)
    last = min(blocks, block + reach + 1)
    return first * LANES, last * LANES


def features(rows, lift_matrix, gain):
    wide = rows.astype(jnp.float32)
    high, rest = split_low(wide * wide)
    stacked = jnp.concatenate([rows, high, rest], axis=1)
    lifted = jnp.dot(stacked, lift_matrix, preferred_element_type=jnp.float32)
    return jnp.exp(lifted) * gain


def strip(entry_row):
    return pltpu.roll(
        jnp.broadcast_to(entry_row, (LANES, entry_row.shape[1])), 0, 1, stride=1, stride_axis=0
    )


def unstrip(total):
    width = total.shape[1]
    half = total.shape[0] // 2
    while half >= 8:
        total = total[:half] + pltpu.roll(total[half:], width - half, 1)
        half //= 2
    row = lax.broadcasted_iota(jnp.int32, total.shape, 0)
    for step in (4, 2, 1):
        total = jnp.where((row & step) != 0, pltpu.roll(total, width - step, 1), total)
    return jnp.sum(total, axis=0, keepdims=True)


def masked_strip(strip_ref, head, seg_col, seg_row, block, blocks, reach):
    first, last = key_span(block, blocks, reach)
    shift = (blocks - 1 - block) * LANES
    columns = seg_col[block * LANES : (block + 1) * LANES]
    same = jnp.concatenate(
        [
            columns == seg_row[:, start : start + LANES]
            for start in range(first, last, LANES)
        ],
        axis=1,
    )
    return jnp.where(same, strip_ref[head, :, first + shift : last + shift], 0.0)


def attend_kernel(
    head_size, reach, q_ref, k_ref, v_ref, col_ref, row_ref, lift_ref, entry_ref,
    mixed_ref, inverse_ref, strip_ref,
):
    length = q_ref.shape[0]
    blocks = length // LANES
    gain = head_size ** (-0.5)
    for head in range(2):
        strip_ref[head] = strip(entry_ref[0, head : head + 1])
    lift_matrix = lift_ref[0]
    query_low = features(q_ref[...], lift_matrix, gain).astype(LOW)
    key_low = features(k_ref[...], lift_matrix, gain).astype(LOW)
    extended = jnp.concatenate([v_ref[...], jnp.ones((length, LANES), LOW)], axis=1)
    lane = lax.broadcasted_iota(jnp.int32, (LANES, LANES), 1)
    seg_row = row_ref[0]
    seg_col = col_ref[0]
    for block in range(blocks):
        first, last = key_span(block, blocks, reach)
        here = slice(block * LANES, (block + 1) * LANES)
        outs = []
        for head in range(2):
            mine = (lane < head_size) == (head == 0)
            block_query = jnp.where(mine, query_low[here], jnp.zeros((), LOW))
            kernel = dot_last(block_query, key_low[first:last])
            weights = kernel * masked_strip(strip_ref, head, seg_col, seg_row, block, blocks, reach)
            outs.append(
                jnp.dot(
                    weights.astype(LOW), extended[first:last], preferred_element_type=jnp.float32
                )
            )
        both = jnp.where(
            jnp.concatenate([lane, lane], axis=1) % LANES < head_size, outs[0], outs[1]
        )
        inverse = 1.0 / both[:, LANES:]
        mixed_ref[here, :] = (both[:, :LANES] * inverse).astype(LOW)
        inverse_ref[here, :] = inverse


def attend_back_kernel(
    head_size, reach, q_ref, k_ref, v_ref, g_ref, mixed_ref, inverse_ref, col_ref, row_ref,
    lift_ref, back_ref, sums_ref, entry_ref,
    gq_ref, gk_ref, gv_ref, logit_ref, strip_ref, diag_ref, value_acc, key_acc,
):
    length = q_ref.shape[0]
    blocks = length // LANES
    gain = head_size ** (-0.5)
    for head in range(2):
        strip_ref[head] = strip(entry_ref[0, head : head + 1])

    @pl.when(pl.program_id(1) == 0)
    def _():
        diag_ref[...] = jnp.zeros_like(diag_ref)

    lift_matrix = lift_ref[0]
    query_feat = features(q_ref[...], lift_matrix, gain)
    key_feat = features(k_ref[...], lift_matrix, gain)
    query_low = query_feat.astype(LOW)
    key_low = key_feat.astype(LOW)
    values = v_ref[...]
    grad_numer = g_ref[...].astype(jnp.float32) * inverse_ref[...]
    grad_low = grad_numer.astype(LOW)
    high, rest = split_low(grad_numer * mixed_ref[...].astype(jnp.float32))
    grad_denom = jnp.dot(
        jnp.concatenate([high, rest], axis=1), sums_ref[...], preferred_element_type=jnp.float32
    )
    lane = lax.broadcasted_iota(jnp.int32, (LANES, LANES), 1)
    seg_row = row_ref[0]
    seg_col = col_ref[0]
    value_acc[...] = jnp.zeros_like(value_acc)
    key_acc[...] = jnp.zeros_like(key_acc)
    grad_qfeat = []
    for block in range(blocks):
        first, last = key_span(block, blocks, reach)
        shift = (blocks - 1 - block) * LANES
        here = slice(block * LANES, (block + 1) * LANES)
        outs = []
        for head in range(2):
            mine = (lane < head_size) == (head == 0)
            block_query = jnp.where(mine, query_low[here], jnp.zeros((), LOW))
            block_grad = jnp.where(mine, grad_low[here], jnp.zeros((), LOW))
            table = masked_strip(strip_ref, head, seg_col, seg_row, block, blocks, reach)
            weights = dot_last(block_query, key_low[first:last]) * table
            denom = grad_denom[here, head * LANES : (head + 1) * LANES]
            grad_weights = dot_last(block_grad, values[first:last]) - jnp.concatenate(
                [denom] * ((last - first) // LANES), axis=1
            )
            grad_kernel = (grad_weights * table).astype(LOW)
            diag_ref[head, :, first + shift : last + shift] += grad_weights * weights
            value_acc[first:last] += dot_first(weights.astype(LOW), block_grad)
            outs.append(
                jnp.dot(grad_kernel, key_low[first:last], preferred_element_type=jnp.float32)
            )
            key_acc[first:last] += dot_first(grad_kernel, block_query)
        grad_qfeat.append(jnp.where(lane < head_size, outs[0], outs[1]))
    gv_ref[...] = value_acc[...].astype(LOW)

    def lift_back(rows, feature, grad_feature):
        product = grad_feature * feature
        high, rest = split_low(product)
        both = jnp.dot(
            jnp.concatenate([high, rest], axis=1), back_ref[0], preferred_element_type=jnp.float32
        )
        return (both[:, :LANES] - rows.astype(jnp.float32) * both[:, LANES:]).astype(LOW)

    gq_ref[...] = lift_back(q_ref[...], query_feat, jnp.concatenate(grad_qfeat, axis=0))
    gk_ref[...] = lift_back(k_ref[...], key_feat, key_acc[...])
    logit_ref[0] = jnp.concatenate([unstrip(diag_ref[head]) for head in range(2)], axis=0)


def pair_matrices(projection):
    heads, head_size, feat = projection.shape
    pairs = projection.reshape(heads // 2, 2, head_size, feat)
    zero = jnp.zeros_like(pairs[:, 0])
    top = jnp.concatenate([pairs[:, 0], zero], axis=2)
    bottom = jnp.concatenate([zero, pairs[:, 1]], axis=2)
    diagonal = jnp.concatenate([top, bottom], axis=1)
    half = jnp.arange(2 * head_size) // head_size
    ones = jnp.broadcast_to(
        (half[:, None] == half[None, :]).astype(LOW), (heads // 2, 2 * head_size, 2 * feat)
    )
    lift_matrix = jnp.concatenate([diagonal, -0.5 * ones, -0.5 * ones], axis=1).astype(LOW)
    turned = jnp.swapaxes(diagonal, 1, 2)
    back_matrix = jnp.concatenate(
        [
            jnp.concatenate([turned, ones], axis=2),
            jnp.concatenate([jnp.zeros_like(turned), ones], axis=2),
        ],
        axis=1,
    )
    picked = (half[:, None] == (jnp.arange(4 * head_size) // (2 * head_size))[None, :]).astype(LOW)
    sums = jnp.concatenate([picked, picked], axis=0)
    return lift_matrix, back_matrix, sums


def entry_rows(position_logits):
    heads, span = position_logits.shape
    entries = jnp.exp(position_logits.astype(jnp.float32))
    padded = jnp.concatenate([entries, jnp.zeros((heads, 1), jnp.float32)], axis=1)
    turned = jnp.roll(padded[:, ::-1], -LANES, axis=1)
    return turned.reshape(heads // 2, 2, span + 1)


def entry_grads(turned):
    pairs, _, width = turned.shape
    flat = turned.reshape(2 * pairs, width)
    return jnp.roll(flat[:, ::-1], -LANES, axis=1)[:, : width - 1]


def attend(queries, keys, values, seg_col, seg_row, lift_matrix, entries, head_size, reach, rows):
    total, width = queries.shape
    length = total // rows
    pairs = width // LANES
    tile = pl.BlockSpec((length, LANES), lambda p, r: (r, p))
    specs = [
        tile, tile, tile,
        pl.BlockSpec((1, length, LANES), lambda p, r: (r, 0, 0)),
        pl.BlockSpec((1, 1, length), lambda p, r: (r, 0, 0)),
        pl.BlockSpec((1,) + lift_matrix.shape[1:], lambda p, r: (p, 0, 0)),
        pl.BlockSpec((1,) + entries.shape[1:], lambda p, r: (p, 0, 0)),
    ]
    return pl.pallas_call(
        functools.partial(attend_kernel, head_size, reach),
        grid=(pairs, rows),
        in_specs=specs,
        out_specs=[tile, tile],
        out_shape=[
            jax.ShapeDtypeStruct((total, width), LOW),
            jax.ShapeDtypeStruct((total, width), jnp.float32),
        ],
        scratch_shapes=[pltpu.VMEM((2, LANES, entries.shape[2]), jnp.float32)],
        name="attend",
    )(queries, keys, values, seg_col, seg_row, lift_matrix, entries)


def attend_back(
    queries, keys, values, grads, mixed, inverse, seg_col, seg_row, lift_matrix, back_matrix,
    sums, entries, head_size, reach, rows,
):
    total, width = queries.shape
    length = total // rows
    pairs = width // LANES
    tile = pl.BlockSpec((length, LANES), lambda p, r: (r, p))
    specs = [
        tile, tile, tile, tile, tile, tile,
        pl.BlockSpec((1, length, LANES), lambda p, r: (r, 0, 0)),
        pl.BlockSpec((1, 1, length), lambda p, r: (r, 0, 0)),
        pl.BlockSpec((1,) + lift_matrix.shape[1:], lambda p, r: (p, 0, 0)),
        pl.BlockSpec((1,) + back_matrix.shape[1:], lambda p, r: (p, 0, 0)),
        pl.BlockSpec(sums.shape, lambda p, r: (0, 0)),
        pl.BlockSpec((1,) + entries.shape[1:], lambda p, r: (p, 0, 0)),
    ]
    low_out = jax.ShapeDtypeStruct((total, width), LOW)
    span = entries.shape[2]
    return pl.pallas_call(
        functools.partial(attend_back_kernel, head_size, reach),
        grid=(pairs, rows),
        in_specs=specs,
        out_specs=[tile, tile, tile, pl.BlockSpec((1, 2, span), lambda p, r: (p, 0, 0))],
        out_shape=[low_out, low_out, low_out, jax.ShapeDtypeStruct((pairs, 2, span), jnp.float32)],
        scratch_shapes=[
            pltpu.VMEM((2, LANES, span), jnp.float32),
            pltpu.VMEM((2, LANES, span), jnp.float32),
            pltpu.VMEM((length, LANES), jnp.float32),
            pltpu.VMEM((length, LANES), jnp.float32),
        ],
        name="attend_back",
    )(
        queries, keys, values, grads, mixed, inverse, seg_col, seg_row, lift_matrix, back_matrix,
        sums, entries,
    )


EPSILON = 1e-05


def normalize(inputs, factor, offset):
    centre = inputs - jnp.mean(inputs, axis=-1, keepdims=True)
    spread = jnp.mean(centre * centre, axis=-1, keepdims=True)
    inverse = lax.rsqrt(spread + EPSILON)
    normed = centre * inverse
    return (normed * factor + offset, normed, inverse)


def norm_back(upstream, normed, inverse, factor):
    scaled = upstream * factor
    inner = (
        scaled
        - jnp.mean(scaled, axis=-1, keepdims=True)
        - normed * jnp.mean(scaled * normed, axis=-1, keepdims=True)
    )
    return (inverse * inner, jnp.sum(upstream * normed, axis=0), jnp.sum(upstream, axis=0))


SWAP = [(0, 1), (1, 0)]
GROUP = ("dp", "mq")


def other(array):
    return lax.ppermute(array, "core", SWAP)


def share_pieces(array):
    piece = array.shape[0] // lax.axis_size("dp")
    mine = lax.dynamic_slice_in_dim(array, lax.axis_index("dp") * piece, piece, 0)
    return lax.all_gather(mine, GROUP, axis=0, tiled=True)


def scatter_pieces(array):
    mine = lax.psum_scatter(array.astype(LOW), GROUP, scatter_dimension=0, tiled=True)
    return lax.all_gather(mine, "dp", axis=0, tiled=True).astype(jnp.float32)


def sum_everywhere(array):
    half = array.shape[0] // 2
    core = lax.axis_index("core")
    low = array.astype(LOW)
    keep = lax.dynamic_slice_in_dim(low, core * half, half, 0)
    give = lax.dynamic_slice_in_dim(low, (1 - core) * half, half, 0)
    pair = (keep.astype(jnp.float32) + other(give).astype(jnp.float32)).astype(LOW)
    mine = lax.psum_scatter(pair, GROUP, scatter_dimension=0, tiled=True)
    whole = lax.all_gather(mine, GROUP, axis=0, tiled=True)
    theirs = other(whole)
    first = jnp.where(core == 0, whole, theirs)
    second = jnp.where(core == 0, theirs, whole)
    return jnp.concatenate([first, second], axis=0).astype(jnp.float32)


def pack_rows(vectors, width, multiple):
    flat = jnp.concatenate([v.reshape(-1) for v in vectors])
    rows = -(-flat.shape[0] // (width * multiple)) * multiple
    return jnp.pad(flat, (0, rows * width - flat.shape[0])).reshape(rows, width)


def unpack_rows(packed, shapes):
    flat = packed.reshape(-1)
    out, at = [], 0
    for shape in shapes:
        size = 1
        for extent in shape:
            size *= extent
        out.append(flat[at : at + size].reshape(shape))
        at += size
    return out


def local(
    tokens,
    segment_ids,
    swap_step,
    feature_bank,
    query_weight,
    query_bias,
    key_weight,
    value_weight,
    value_bias,
    out_weight,
    out_bias,
    position_logits,
    first_gain,
    first_shift,
    up_weight,
    up_bias,
    down_weight,
    down_bias,
    second_gain,
    second_shift,
    out_cotangent,
):
    rows_here, length, model_width = tokens.shape
    head_count = position_logits.shape[0]
    head_size = model_width // head_count
    query_scale = head_size ** (-0.25)
    hidden_here = up_weight.shape[1]
    token_rows = tokens.reshape(-1, model_width)
    token_count = token_rows.shape[0]
    core = lax.axis_index("core")

    up_turned = share_pieces(up_weight.T)
    down = share_pieces(down_weight)
    up_bias_here = share_pieces(up_bias[:, None])[:, 0].astype(jnp.float32)

    projection = lax.dynamic_index_in_dim(
        feature_bank, swap_step[0] % feature_bank.shape[0], 0, keepdims=False
    )
    lift_matrix, back_matrix, sums = pair_matrices(projection)
    entries = entry_rows(position_logits)
    seg_col = jnp.broadcast_to(segment_ids[:, :, None], (rows_here, length, LANES))
    seg_row = segment_ids[:, None, :]

    queries = (
        (
            jnp.dot(token_rows, query_weight, preferred_element_type=jnp.float32)
            + query_bias.astype(jnp.float32)
        )
        * query_scale
    ).astype(LOW)
    keys_all = (
        jnp.dot(token_rows, key_weight, preferred_element_type=jnp.float32) * query_scale
    ).astype(LOW)
    values = (
        jnp.dot(token_rows, value_weight, preferred_element_type=jnp.float32)
        + value_bias.astype(jnp.float32)
    ).astype(LOW)
    mixed_out, inverse = attend(
        queries, keys_all, values, seg_col, seg_row, lift_matrix, entries, head_size, REACH,
        rows_here,
    )
    branch = jnp.dot(mixed_out, out_weight, preferred_element_type=jnp.float32) + out_bias.astype(
        jnp.float32
    )
    first_factor = first_gain.astype(jnp.float32)
    hidden, first_normed, first_inverse = normalize(
        token_rows.astype(jnp.float32) + branch, first_factor, first_shift.astype(jnp.float32)
    )
    hidden_low = hidden.astype(LOW)
    hidden_pair = jnp.concatenate([hidden_low, other(hidden_low)], axis=0)
    upward = dot_last(hidden_pair, up_turned) + up_bias_here
    activated = jax.nn.gelu(upward, approximate=False).astype(LOW)
    theirs = jnp.dot(activated[token_count:], down, preferred_element_type=jnp.float32)
    feed_out = jnp.dot(
        activated[:token_count], down, preferred_element_type=jnp.float32
    ) + other(theirs)
    second_factor = second_gain.astype(jnp.float32)
    summed = hidden + feed_out + down_bias.astype(jnp.float32)
    layer_out, second_normed, second_inverse = normalize(
        summed, second_factor, second_shift.astype(jnp.float32)
    )
    upstream = out_cotangent.reshape(-1, model_width).astype(jnp.float32)
    grad_summed, grad_second_gain, grad_second_shift = norm_back(
        upstream, second_normed, second_inverse, second_factor
    )
    grad_down_bias = jnp.sum(grad_summed, axis=0)
    grad_feed = grad_summed.astype(LOW)

    def gelu_exact(inputs):
        return jax.nn.gelu(inputs, approximate=False)

    grad_pair = jnp.concatenate([grad_feed, other(grad_feed)], axis=0)
    part_down_weight = dot_first(activated, grad_pair)
    grad_down_weight = scatter_pieces(part_down_weight)
    grad_act = dot_last(grad_pair, down)
    grad_upward = jax.vjp(gelu_exact, upward)[1](grad_act)[0].astype(LOW)
    part_up_turned = dot_first(grad_upward, hidden_pair)
    grad_up_weight = scatter_pieces(part_up_turned).T
    part_up_bias = jnp.sum(grad_upward.astype(jnp.float32), axis=0)
    back_theirs = jnp.dot(
        grad_upward[token_count:], up_turned, preferred_element_type=jnp.float32
    )
    grad_hidden = (
        grad_summed
        + jnp.dot(grad_upward[:token_count], up_turned, preferred_element_type=jnp.float32)
        + other(back_theirs)
    )
    grad_residual, grad_first_gain, grad_first_shift = norm_back(
        grad_hidden, first_normed, first_inverse, first_factor
    )
    grad_branch = grad_residual.astype(LOW)
    grad_out_bias = jnp.sum(grad_branch.astype(jnp.float32), axis=0)
    grad_out_weight = dot_first(mixed_out, grad_branch)
    grad_mixed = dot_last(grad_branch, out_weight).astype(LOW)
    multiple = 2 * lax.axis_size(GROUP)
    bias_pair = jnp.zeros((2,) + part_up_bias.shape, jnp.float32).at[core].set(part_up_bias)
    early = [
        grad_out_bias,
        grad_first_gain,
        grad_first_shift,
        grad_down_bias,
        grad_second_gain,
        grad_second_shift,
        bias_pair,
    ]
    early_sum = sum_everywhere(
        jnp.concatenate([grad_out_weight, pack_rows(early, model_width, multiple)], axis=0)
    )

    grad_queries, grad_keys, grad_values, turned_logits = attend_back(
        queries, keys_all, values, grad_mixed, mixed_out, inverse, seg_col, seg_row, lift_matrix,
        back_matrix, sums, entries, head_size, REACH, rows_here,
    )
    grad_query_weight = dot_first(token_rows, grad_queries) * query_scale
    grad_query_bias = jnp.sum(grad_queries.astype(jnp.float32), axis=0) * query_scale
    grad_key_weight = dot_first(token_rows, grad_keys) * query_scale
    grad_value_weight = dot_first(token_rows, grad_values)
    grad_value_bias = jnp.sum(grad_values.astype(jnp.float32), axis=0)
    late = [grad_query_bias, grad_value_bias, turned_logits]
    late_sum = sum_everywhere(
        jnp.concatenate(
            [
                grad_query_weight,
                grad_key_weight,
                grad_value_weight,
                pack_rows(late, model_width, multiple),
            ],
            axis=0,
        )
    )
    grad_tokens = (
        grad_residual
        + query_scale * (dot_last(grad_queries, query_weight) + dot_last(grad_keys, key_weight))
        + dot_last(grad_values, value_weight)
    )
    early_out = unpack_rows(early_sum[model_width:], [v.shape for v in early])
    late_out = unpack_rows(late_sum[3 * model_width :], [v.shape for v in late])
    pieces = lax.axis_size("dp")
    bias_all = early_out[6].reshape(2, pieces, lax.axis_size("mq"), hidden_here // pieces)
    grad_up_bias = lax.dynamic_index_in_dim(
        lax.dynamic_index_in_dim(bias_all, core, 0, keepdims=False),
        lax.axis_index("mq"),
        1,
        keepdims=False,
    ).reshape(-1)
    return (
        layer_out.astype(LOW).reshape(rows_here, length, model_width),
        grad_tokens.reshape(rows_here, length, model_width),
        late_sum[:model_width],
        late_out[0],
        late_sum[model_width : 2 * model_width],
        late_sum[2 * model_width : 3 * model_width],
        late_out[1],
        early_sum[:model_width],
        early_out[0],
        entry_grads(late_out[2]),
        early_out[1],
        early_out[2],
        grad_up_weight,
        grad_up_bias,
        grad_down_weight,
        early_out[3],
        early_out[4],
        early_out[5],
    )


REACH = 2


def solution(mesh):
    groups, parts = mesh.devices.shape
    cores = jax.sharding.Mesh(mesh.devices.reshape(groups, parts // 2, 2), ("dp", "mq", "core"))
    rows = ("dp", "mq", "core")
    units = ("mq", "core")
    whole = P()
    in_specs = (
        (P(rows, None, None), P(rows, None))
        + (whole,) * 12
        + (P(None, units), P(units), P(units, None))
        + (whole,) * 3
        + (P(rows, None, None),)
    )
    out_specs = (
        (P(rows, None, None), P(rows, None, None))
        + (whole,) * 10
        + (P(None, units), P(units), P(units, None))
        + (whole,) * 3
    )
    return jax.shard_map(local, mesh=cores, in_specs=in_specs, out_specs=out_specs, check_vma=False)
```

time: 1380 us -> 662 us (0.48)
  waiting for transfers between devices: 860 us -> 287 us
  local copies, waits for them, and re-layouts: 320 us -> 32.6 us
  blocking collectives: 5.64 us -> 156 us
  matrix products: 142 us -> 78.9 us
  Pallas kernels: 0 us -> 31 us
  starting transfers between devices: 0.69 us -> 24.9 us
    reduce_scatter x2, waiting for transfers between devices: 481 us -> 204 us  [scatter_pieces(): lax.psum_scatter(array.astype(LOW), GROUP, scatter_dimension=0, tiled=True)]
    psum x3 -> x0, waiting for transfers between devices: 177 us -> none  [the longest x2 141 us: local(): lax.psum((grad_query_weight, grad_query_bias, grad_key_weight, grad_value...]
    reshape x3 -> x5, local copies, waits for them, and re-layouts: 133 us -> 2.07 us  [the longest x2 0.75 us: pack_rows(): return jnp.pad(flat, (0, rows * width - flat.shape[0])).reshape(rows, width)]
    all_gather x2 -> x3, waiting for transfers between devices: 201 us -> 72.7 us  [the longest x2 45.1 us: share_pieces(): return lax.all_gather(mine, GROUP, axis=0, tiled=True)]
    unnamed x0 -> x2, blocking collectives: none -> 100 us
    dot_general x12 -> x4, matrix products: 74.1 us -> 12.9 us  [the longest x1 5.02 us: local(): jnp.dot(grad_upward[:token_count], up_turned, preferred_element_type=jnp....]
    all_gather x0 -> x3, blocking collectives: none -> 55.6 us  [the longest x1 43.6 us: sum_everywhere(): whole = lax.all_gather(mine, GROUP, axis=0, tiled=True)]
    another operation x2 -> x4, local copies, waits for them, and re-layouts: 49.6 us -> 0.18 us  [toeplitz(): tiled = jnp.tile(rolled, (1, length))[:, :length * (span - 1)]]
  transfers between devices with their start and end apart: 7 -> 19, of which waited for: 7 -> 10; matrix products, arithmetic and copies ran while one was open for 14% -> 11% of each run, Pallas kernels for 0% -> 1%
where the time goes in v1:
time: 662 us; the launch traced here: 655 us
  waiting for transfers between devices  287 us (43%)
  blocking collectives  156 us (24%)
  matrix products  78.9 us (12%)
  local copies, waits for them, and re-layouts  32.6 us (5%)
  Pallas kernels  31 us (5%)
  other arithmetic  26.7 us (4%)
  starting transfers between devices  24.9 us (4%)
  between operations  17 us (3%)
    reduce_scatter x2, waiting for transfers between devices, scatter_pieces(): lax.psum_scatter(array.astype(LOW), GROUP, scatter_dimension=0, tiled=True)  204 us
    unnamed x2, blocking collectives  100 us
    all_gather x2, waiting for transfers between devices, share_pieces(): return lax.all_gather(mine, GROUP, axis=0, tiled=True)  45.1 us
    all_gather x1, blocking collectives, sum_everywhere(): whole = lax.all_gather(mine, GROUP, axis=0, tiled=True)  43.6 us
    dot_general x6, matrix products, dot_last(): lax.dot_general(left_side, right_side, (((1,), (1,)), ((), ())), preferre...  37.6 us
    all_gather x1, waiting for transfers between devices, sum_everywhere(): whole = lax.all_gather(mine, GROUP, axis=0, tiled=True)  27.6 us
    unnamed x6, starting transfers between devices  23.7 us
    pallas_call x1, Pallas kernels, attend_back(): pl.pallas_call(functools.partial(attend_back_kernel, head_size, reach), g...  21.5 us
  transfers between devices with their start and end apart: 19, of which 10 were waited for; matrix products, arithmetic and copies ran while one was open for 11% of the time, Pallas kernels for 1%

profile of v1, /device:TPU:8, one launch (start us, length us, event | category | flops | bytes accessed | tf_op | source)
XLA Modules:
  0.0 654.6 jit_solution(13169942454147614933)
XLA Ops:
  13.4 2.9 multiply_convert_fusion.3.k_ref
  20.5 9.6 %attend.1 = (bf16[512,768]{1,0:T(8,128)(2,1)}, f32[512,768]{1,0:T(8,128)}) custom-call(bf16[512,768]{1,0:T(8,128)(2,1)} %multiply_convert_fusion.4.q_ref, bf16[512,768]{1,0:T(8,128)(2,1)} %multiply_convert_fusion.3.k_ref, bf16[512,768]{1,0:T(8,128)(2,1)} %add_convert_fusion.3.v_ref, s32[1,512,128]{2,1,0:T(8,128)} %broadcast_in_dim.17.col_ref, ...), custom_call_target="tpu_custom_call" | custom-call | tf_op jit(solution)/shard_map/attend/pallas_call | solution.py:236
  35.6 38.9 %all-reduce.6 = bf16[1536]{0:T(1024)(128)(2,1)S(1)} all-reduce(bf16[1536]{0:T(1024)(128)(2,1)S(1)} %dynamic-update-slice.3), channel_id=2, replica_groups=mesh['dp'=2,'mq'=8,'core'=2] {'dp','mq'}, use_global_device_ids=true, to_apply=%add.6 | all-reduce | flops 1536 | bytes 6144
  75.1 19.5 %multiply_convert_fusion = (bf16[1024,1536]{1,0:T(8,128)(2,1)}, f32[1024,1536]{1,0:T(8,128)}, f32[1024,1536]{1,0:T(8,128)}) fusion(f32[1536]{0:T(1024)S(1)} %convert_element_type.175, bf16[1536,768]{1,0:T(8,128)(2,1)} %all-gather.7.cloned.1.call-done, bf16[512,768]{1,0:T(8,128)(2,1)} %collective-permute-done, bf16[512,768]{1,0:T(8,128)(2,1)S(1)} %fusion.31), kind=kOutput, calls=%fused_computation.4 | convolution fusion | flops 2522873856 | bytes 19666944 | tf_op jit(solution)/shard_map/dot_general | solution.py:14
  94.7 44.5 %all-gather.9.cloned.1.call-done = bf16[1536,768]{1,0:T(8,128)(2,1)} async-done(((bf16[96,768]{1,0:T(8,128)(2,1)}), bf16[1536,768]{1,0:T(8,128)(2,1)}) %all-gather.9.cloned.1.call-update) | async-done | bytes 2359312 | tf_op jit(solution)/shard_map/all_gather | solution.py:320
  139.2 3.7 fusion.19
  143.0 3.3 collective-permute-done.1
  156.2 8.7 %convert_reduce_fusion = (bf16[1536]{0:T(1024)(128)(2,1)}, bf16[1024,1536]{1,0:T(8,128)(2,1)S(1)}) fusion(f32[1024,1536]{1,0:T(8,128)S(1)} %bitcast.93, bf16[1536,768]{1,0:T(8,128)(2,1)S(1)} %copy-done.50, bf16[512,768]{1,0:T(8,128)(2,1)S(1)} %collective-permute-done.2, bf16[512,768]{1,0:T(8,128)(2,1)S(1)} %convert_element_type.154, ...), kind=kOutput, calls=%fused_computation.2 | convolution fusion | flops 2445801984 | bytes 19670016 | tf_op jit(solution)/shard_map/dot_general | solution.py:14
  164.9 2.5 fusion.15
  171.2 5.0 multiply_reduce_fusion
  179.3 21.5 %attend_back.1 = (bf16[512,768]{1,0:T(8,128)(2,1)}, bf16[512,768]{1,0:T(8,128)(2,1)}, bf16[512,768]{1,0:T(8,128)(2,1)}, f32[6,2,1024]{2,1,0:T(2,128)}) custom-call(bf16[512,768]{1,0:T(8,128)(2,1)} %multiply_convert_fusion.4.q_ref, bf16[512,768]{1,0:T(8,128)(2,1)} %multiply_convert_fusion.3.k_ref, bf16[512,768]{1,0:T(8,128)(2,1)} %add_convert_fusion.3.v_ref, ...), custom_call_target="tpu_custom_call" | custom-call | tf_op jit(solution)/shard_map/attend_back/pallas_call | solution.py:269
  202.1 2.3 fusion.28
  206.6 2.3 fusion.30
  221.8 2.5 add_convert_fusion.1
  224.2 61.6 %fusion.56 = (bf16[80,768]{1,0:T(8,128)(2,1)S(1)}, bf16[32,768]{1,0:T(8,128)(2,1)S(1)}) fusion(bf16[1168,768]{1,0:T(8,128)(2,1)S(1)} %add_convert_fusion.1, bf16[400,768]{1,0:T(8,128)(2,1)} %add_convert_fusion.4), kind=kCustom, calls=%all-reduce-scatter.2 | all-reduce-scatter fusion | flops 1376258 | bytes 2580992
  285.9 2.3 collective-permute-start.8
  288.2 4.8 collective-permute-start.9
  296.1 6.4 convolution_convert_fusion
  303.6 6.2 convolution_convert_fusion.1
  309.8 3.5 collective-permute-start.10
  313.4 4.6 collective-permute-start.11
  318.0 6.4 collective-permute-start.12
  326.4 3.2 fusion.65
  330.5 27.6 %all-gather.11.cloned.1.call-done = bf16[16,73,768]{2,1,0:T(8,128)(2,1)} async-done(((bf16[1,73,768]{2,1,0:T(8,128)(2,1)}), bf16[16,73,768]{2,1,0:T(8,128)(2,1)}) %all-gather.11.cloned.1.call-update) | async-done | bytes 1794064 | tf_op jit(solution)/shard_map/all_gather | solution.py:336
  360.0 43.6 %all-gather.2 = bf16[16,25,768]{2,1,0:T(8,128)(2,1)} all-gather(bf16[1,25,768]{2,1,0:T(8,128)(2,1)S(1)} %dynamic-slice_bitcast_fusion.2), channel_id=1, replica_groups=mesh['dp'=2,'mq'=8,'core'=2] {'dp','mq'}, dimensions={0}, use_global_device_ids=true | all-gather | bytes 652800 | tf_op jit(solution)/shard_map/all_gather | solution.py:336
  405.8 2.5 fusion.66
  413.7 78.1 %reduce-scatter.9.cloned.1.call-done = bf16[96,768]{1,0:T(8,128)(2,1)} async-done(((bf16[1536,768]{1,0:T(8,128)(2,1)}), bf16[96,768]{1,0:T(8,128)(2,1)}) %reduce-scatter.9.cloned.1.call-update) | async-done | bytes 147472 | tf_op jit(solution)/shard_map/reduce_scatter | solution.py:324
  491.7 6.0 all_gather.27
  498.6 126.3 %reduce-scatter.7.cloned.1.call-done = bf16[96,768]{1,0:T(8,128)(2,1)} async-done(((bf16[1536,768]{1,0:T(8,128)(2,1)}), bf16[96,768]{1,0:T(8,128)(2,1)}) %reduce-scatter.7.cloned.1.call-update) | async-done | bytes 147472 | tf_op jit(solution)/shard_map/reduce_scatter | solution.py:324
  624.9 6.0 all_gather.26
  636.9 3.4 maximum_convert_fusion
  640.9 6.3 fusion.60
  (279 shorter events, 71.5 us)
Async XLA Ops:
  7.3 67.9 %all-gather.7.cloned.1.call-start = ((), (), s32[]{:S(2)}) async-start(), calls=%async_computation.2 | async-start | bytes 2506752 | tf_op jit(solution)/shard_map/all_gather | solution.py:320
  9.0 130.1 %all-gather.9.cloned.1.call-start = ((), (), s32[]{:S(2)}) async-start(), calls=%async_computation.3 | async-start | bytes 2506752 | tf_op jit(solution)/shard_map/all_gather | solution.py:320
  11.8 20.8 %copy-start.28 = (f32[768]{0:T(1024)}, f32[768]{0:T(1024)S(1)}, u32[]{:S(2)}) copy-start(f32[768]{0:T(1024)S(1)} %convert_element_type.143) | copy-start | bytes 9220
  19.7 10.4 %copy-start.51 = (bf16[768,768]{1,0:T(8,128)(2,1)S(1)}, bf16[768,768]{1,0:T(8,128)(2,1)}, u32[]{:S(2)}) copy-start(bf16[768,768]{1,0:T(8,128)(2,1)} %param.32) | copy-start | bytes 3538948
  33.0 61.7 %copy-start.19 = (bf16[512,768]{1,0:T(8,128)(2,1)}, bf16[512,768]{1,0:T(8,128)(2,1)S(1)}, u32[]{:S(2)}) copy-start(bf16[512,768]{1,0:T(8,128)(2,1)S(1)} %fusion.31) | copy-start | bytes 2359300
  33.0 41.5 %collective-permute-start = (bf16[512,768]{1,0:T(8,128)(2,1)S(1)}, bf16[512,768]{1,0:T(8,128)(2,1)}, u32[]{:S(2)}, u32[]{:S(2)}) collective-permute-start(bf16[512,768]{1,0:T(8,128)(2,1)S(1)} %fusion.31), channel_id=1, source_target_pairs={{0,1},{1,0},{2,3},{3,2},{4,5},{5,4},{6,7},{7,6},{8,9},{9,8},{10,11... | collective-permute-start | bytes 2359304 | tf_op jit(solution)/shard_map/ppermute | solution.py:314
  34.0 324.1 %all-gather.11.cloned.1.call-start = ((), (), s32[]{:S(2)}) async-start(), calls=%async_computation.6 | async-start | bytes 2088960 | tf_op jit(solution)/shard_map/all_gather | solution.py:336
  74.5 20.1 %copy-start.33 = (f32[1536]{0:T(1024)}, f32[1536]{0:T(1024)S(1)}, u32[]{:S(2)}) copy-start(f32[1536]{0:T(1024)S(1)} %convert_element_type.175) | copy-start | bytes 18436
  139.1 7.2 %copy-start.29 = (f32[768]{0:T(1024)S(1)}, f32[768]{0:T(1024)}, u32[]{:S(2)}) copy-start(f32[768]{0:T(1024)} %copy-done.28) | copy-start | bytes 9220
  139.1 7.2 %copy-start.50 = (bf16[1536,768]{1,0:T(8,128)(2,1)S(1)}, bf16[1536,768]{1,0:T(8,128)(2,1)}, u32[]{:S(2)}) copy-start(bf16[1536,768]{1,0:T(8,128)(2,1)} %all-gather.9.cloned.1.call-done) | copy-start | bytes 7077892
  139.1 17.1 %slice-start = ((s8[6291456]{0:T(1024)(128)(4,1)}), s8[4194304]{0:T(1024)(128)(4,1)S(1)}, s32[]{:S(2)}) async-start(s8[6291456]{0:T(1024)(128)(4,1)} %bitcast.92), calls=%async_computation.7 | async-start | bytes 8388608
  142.8 3.5 collective-permute-start.1
  143.0 13.2 %slice-start.1 = ((s8[6291456]{0:T(1024)(128)(4,1)}), s8[2097152]{0:T(1024)(128)(4,1)S(1)}, s32[]{:S(2)}) async-start(s8[6291456]{0:T(1024)(128)(4,1)} %bitcast.92), calls=%async_computation.8 | async-start | bytes 4194304
  153.8 11.1 %copy-start.21 = (bf16[512,768]{1,0:T(8,128)(2,1)}, bf16[512,768]{1,0:T(8,128)(2,1)S(1)}, u32[]{:S(2)}) copy-start(bf16[512,768]{1,0:T(8,128)(2,1)S(1)} %convert_element_type.154) | copy-start | bytes 2359300
  153.9 2.4 collective-permute-start.2
  156.2 8.7 %copy-start.57 = (bf16[512,768]{1,0:T(8,128)(2,1)}, bf16[512,768]{1,0:T(8,128)(2,1)S(1)}, u32[]{:S(2)}) copy-start(bf16[512,768]{1,0:T(8,128)(2,1)S(1)} %collective-permute-done.2) | copy-start | bytes 2359300
  156.2 8.7 %copy-start.49 = (bf16[1536,768]{1,0:T(8,128)(2,1)S(1)}, bf16[1536,768]{1,0:T(8,128)(2,1)}, u32[]{:S(2)}) copy-start(bf16[1536,768]{1,0:T(8,128)(2,1)} %all-gather.7.cloned.1.call-done) | copy-start | bytes 7077892
  167.5 3.8 collective-permute-start.3
  211.8 10.0 %collective-permute-start.4 = (bf16[1168,768]{1,0:T(8,128)(2,1)}, bf16[1168,768]{1,0:T(8,128)(2,1)}, u32[]{:S(2)}, u32[]{:S(2)}) collective-permute-start(bf16[1168,768]{1,0:T(8,128)(2,1)} %constant_dynamic-slice_fusion.1), channel_id=1, source_target_pairs={{0,1},{1,0},{2,3},{3,2},{4,5},{5,4},{6,7},{7,6},{8,9},{9,8},{10,11... | collective-permute-start | bytes 5382152 | tf_op jit(solution)/shard_map/ppermute | solution.py:314
  218.2 2.2 collective-permute-start.6
  285.9 8.9 %collective-permute-start.8 = (bf16[80,768]{1,0:T(8,128)(2,1)S(1)}, bf16[80,768]{1,0:T(8,128)(2,1)S(1)}, u32[]{:S(2)}, u32[]{:S(2)}) collective-permute-start(bf16[80,768]{1,0:T(8,128)(2,1)S(1)} %get-tuple-element.59), channel_id=1, source_target_pairs={{0,2},{2,4},{4,6},{6,8},{8,10},{10,12},{12,14},{14,16},{16,18},{18... | collective-permute-start | bytes 368648
  288.2 6.5 %collective-permute-start.9 = (bf16[25,768]{1,0:T(8,128)(2,1)S(1)}, bf16[25,768]{1,0:T(8,128)(2,1)S(1)}, u32[]{:S(2)}, u32[]{:S(2)}) collective-permute-start(bf16[25,768]{1,0:T(8,128)(2,1)S(1)} %slice.192), channel_id=1, source_target_pairs={{0,4},{2,6},{4,8},{6,10},{8,12},{10,14},{12,16},{14,18},{16,20},{1... | collective-permute-start | bytes 115208
  296.1 195.7 %reduce-scatter.9.cloned.1.call-start = ((), (), s32[]{:S(2)}) async-start(), calls=%async_computation.5 | async-start | bytes 2506752 | tf_op jit(solution)/shard_map/reduce_scatter | solution.py:324
  302.5 322.4 %reduce-scatter.7.cloned.1.call-start = ((), (), s32[]{:S(2)}) async-start(), calls=%async_computation.4 | async-start | bytes 2506752 | tf_op jit(solution)/shard_map/reduce_scatter | solution.py:324
  309.8 16.6 %copy-start.18 = (bf16[512,768]{1,0:T(8,128)(2,1)S(1)}, bf16[512,768]{1,0:T(8,128)(2,1)}, u32[]{:S(2)}) copy-start(bf16[512,768]{1,0:T(8,128)(2,1)} %get-tuple-element.38) | copy-start | bytes 2359300
  309.8 19.8 %collective-permute-start.10 = (bf16[32,768]{1,0:T(8,128)(2,1)S(1)}, bf16[32,768]{1,0:T(8,128)(2,1)S(1)}, u32[]{:S(2)}, u32[]{:S(2)}) collective-permute-start(bf16[32,768]{1,0:T(8,128)(2,1)S(1)} %get-tuple-element.60), channel_id=1, source_target_pairs={{0,2},{2,4},{4,6},{6,8},{8,10},{10,12},{12,14},{14,16},{16,18},{18... | collective-permute-start | bytes 147464
  313.4 16.3 %collective-permute-start.11 = (bf16[32,768]{1,0:T(8,128)(2,1)S(1)}, bf16[32,768]{1,0:T(8,128)(2,1)S(1)}, u32[]{:S(2)}, u32[]{:S(2)}) collective-permute-start(bf16[32,768]{1,0:T(8,128)(2,1)S(1)} %get-tuple-element.60), channel_id=1, source_target_pairs={{0,4},{2,6},{4,8},{6,10},{8,12},{10,14},{12,16},{14,18},{16,20},{1... | collective-permute-start | bytes 147464
  318.0 11.6 %collective-permute-start.12 = (bf16[32,768]{1,0:T(8,128)(2,1)S(1)}, bf16[32,768]{1,0:T(8,128)(2,1)S(1)}, u32[]{:S(2)}, u32[]{:S(2)}) collective-permute-start(bf16[32,768]{1,0:T(8,128)(2,1)S(1)} %get-tuple-element.60), channel_id=1, source_target_pairs={{0,6},{2,8},{4,10},{6,12},{8,14},{10,16},{12,18},{14,20},{16,22},{... | collective-permute-start | bytes 147464
  324.4 5.2 collective-permute-start.13
  359.9 48.4 %copy-start.5 = (bf16[1168,768]{1,0:T(8,128)(2,1)}, bf16[1168,768]{1,0:T(8,128)(2,1)S(1)}, u32[]{:S(2)}) copy-start(bf16[1168,768]{1,0:T(8,128)(2,1)S(1)} %reshape.245) | copy-start | bytes 5382148
  359.9 271.9 %collective-permute-start.5 = (bf16[1168,768]{1,0:T(8,128)(2,1)S(1)}, bf16[1168,768]{1,0:T(8,128)(2,1)}, u32[]{:S(2)}, u32[]{:S(2)}) collective-permute-start(bf16[1168,768]{1,0:T(8,128)(2,1)S(1)} %reshape.245), channel_id=1, source_target_pairs={{0,1},{1,0},{2,3},{3,2},{4,5},{5,4},{6,7},{7,6},{8,9},{9,8},{10,11... | collective-permute-start | bytes 5382152 | tf_op jit(solution)/shard_map/ppermute | solution.py:314
  405.8 4.6 collective-permute-start.7
  (50 other events, 153.0 us)
Sparse Core Ops, SparseCore 0:
  11.3 63.7 all-gather.6
  78.4 60.6 all-gather.8
  296.2 61.8 all-gather.10
  363.5 128.2 reduce-scatter.8
  497.1 127.8 reduce-scatter.6
